TPU v7x, 512 devices: a whole 4x4x16 slice. The times are simulated.
512 devices in a mesh: src: 64 (over z, x), tm: 8 (over y, core).
Axes of the slice: x: 4, y: 4, z: 16, core: 2. Of those that a mesh axis runs over, the one named last changes fastest.
Arguments:
- left_vector: float32 [8, 131072], P(None, ('src', 'tm')), may hold values from -12 to 12
- source_coeffs: float32 [5, 8, 131072], P(None, None, ('src', 'tm')), may hold values from -1.5 to 1.5
- knot_coeffs: float32 [12, 8, 131072], P(None, None, ('src', 'tm')), may hold values from -1.5 to 1.5
- source_index: int32 [8, 131072], P(None, ('src', 'tm')), may hold values from 0 to 1023
- band_start: int32 [8, 131072], P(None, ('src', 'tm')), may hold values from 0 to 4095, as said below
- bucket_fill: int32 [8, 512], P(None, ('src', 'tm')), may hold values from 51 to 256, as said below
- source_vector: float32 [5, 524288], P(None, ('src', 'tm')), may hold values from -6 to 6
- knot_vector: float32 [3, 8, 16384], P(None, 'tm', 'src'), may hold values from -6 to 6
- source_search: float32 [5, 524288], P(None, ('src', 'tm')), may hold values from -6 to 6
- knot_search: float32 [3, 8, 16384], P(None, 'tm', 'src'), may hold values from -6 to 6
- source_solution: float32 [5, 524288], P(None, ('src', 'tm')), may hold values from -6 to 6
- knot_solution: float32 [3, 8, 16384], P(None, 'tm', 'src'), may hold values from -6 to 6
- recurrence: float32 [3], replicated, may hold values from 0.5 to 1.5
Outputs:
- left_next: float32 [8, 131072], P(None, ('src', 'tm'))
- source_next: float32 [5, 524288], P(None, ('src', 'tm'))
- knot_next: float32 [3, 8, 16384], P(None, 'tm', 'src')
- search_source: float32 [5, 524288], P(None, ('src', 'tm'))
- search_knot: float32 [3, 8, 16384], P(None, 'tm', 'src')
- solution_source: float32 [5, 524288], P(None, ('src', 'tm'))
- solution_knot: float32 [3, 8, 16384], P(None, 'tm', 'src')
- recurrence_next: float32 [4], replicated
Inputs may be any that keep to these rules, and one draw needn't show every extreme that they name: `bucket_fill`: in every draw one bucket of some group block holds exactly 256 observations. Call band_start // 64 the knot owner of a slot. Among the 8 x 256 slots of one column block of 256, each knot owner is named at most 64 times, and in every block some owner exactly 64 times.
All inputs are finite; a program needn't handle non-finite values.
Results may differ from a plain program's by a relative error of at most 0.00002.
Values sent between devices are 32-bit elements; how exact they have to be, the bound alone decides.
A program may use at most 64 MiB of HBM per device.

v0:
```python
import jax
import jax.numpy as jnp
from jax import lax
from jax.sharding import PartitionSpec as P

KB = 4
EPSILON = 1e-06


def band_positions(band_start, knots_slab):
    rows = jnp.arange(3 * KB, dtype=jnp.int32)
    base = rows // KB * knots_slab + rows % KB
    return base[:, None, None] + KB * band_start[None]


def shards(
    left_vector,
    source_coeffs,
    knot_coeffs,
    source_index,
    band_start,
    bucket_fill,
    source_vector,
    knot_vector,
    source_search,
    knot_search,
    source_solution,
    knot_solution,
    recurrence,
):
    slab_count = lax.axis_size("tm")
    group_count = lax.axis_size("src")
    devices = slab_count * group_count
    buckets, capacity = left_vector.shape
    source_dev = source_vector.shape[1]
    knot_dev = knot_vector.shape[2]
    knots_slab = knot_dev * group_count
    total_obs = buckets * capacity * devices
    unknowns = (5 * source_dev + 3 * knot_dev) * devices
    ratio = unknowns / total_obs
    alpha = recurrence[0]
    pivot = recurrence[1]
    remainder = recurrence[2]
    slot = lax.broadcasted_iota(jnp.int32, (buckets, capacity), 1)
    valid = (slot < bucket_fill).astype(jnp.float32)
    flat_source = source_index.reshape(-1)
    picked = jnp.take(source_vector, flat_source, axis=1).reshape(5, buckets, capacity)
    image = jnp.sum(source_coeffs * picked, axis=0)
    own_knots = knot_vector[:, 0, :]
    slab_whole = lax.all_gather(own_knots, "src", axis=1, tiled=True).reshape(-1)
    positions = band_positions(band_start, knots_slab)
    knot_image = jnp.sum(knot_coeffs * jnp.take(slab_whole, positions), axis=0)
    returned = lax.all_to_all(knot_image, "tm", split_axis=0, concat_axis=0, tiled=True)
    raw = valid * (image + returned - alpha * left_vector)
    own_squares = jnp.sum(raw * raw)
    beta = jnp.sqrt(lax.psum(own_squares, ("src", "tm")) / total_obs + EPSILON)
    outgoing = raw / beta
    arrived = lax.all_to_all(outgoing, "tm", split_axis=0, concat_axis=0, tiled=True)
    gradient_source = (
        jnp.zeros((5, source_dev), jnp.float32)
        .at[:, flat_source]
        .add((source_coeffs * outgoing[None]).reshape(5, -1))
    )
    knot_terms = (
        jnp.zeros((3 * knots_slab,), jnp.float32)
        .at[positions.reshape(-1)]
        .add((knot_coeffs * arrived[None]).reshape(-1))
        .reshape(3, knots_slab)
    )
    knot_totals = lax.psum(knot_terms, "src")
    gradient_knot = lax.dynamic_slice_in_dim(
        knot_totals, lax.axis_index("src") * knot_dev, knot_dev, 1
    )
    source_raw = ratio * gradient_source - beta * source_vector
    knot_raw = ratio * gradient_knot - beta * own_knots
    squares = jnp.sum(source_raw * source_raw) + jnp.sum(knot_raw * knot_raw)
    alpha_next = jnp.sqrt(lax.psum(squares, ("src", "tm")) / unknowns + EPSILON)
    left_next = raw / beta
    source_next = source_raw / alpha_next
    knot_next = knot_raw / alpha_next
    radius = jnp.sqrt(pivot * pivot + beta * beta)
    cosine = pivot / radius
    sine = beta / radius
    coupling = sine * alpha_next
    step_gain = cosine * remainder
    solution_source = source_solution + step_gain / radius * source_search
    solution_knot = knot_solution + step_gain / radius * knot_search
    search_source = source_next - coupling / radius * source_search
    search_knot = knot_next[:, None, :] - coupling / radius * knot_search
    recurrence_next = jnp.stack([alpha_next, beta, -cosine * alpha_next, sine * remainder])
    return (
        left_next,
        source_next,
        knot_next[:, None, :],
        search_source,
        search_knot,
        solution_source,
        solution_knot,
        recurrence_next,
    )


def solution(mesh):
    in_specs = (
        P(None, ("src", "tm")),
        P(None, None, ("src", "tm")),
        P(None, None, ("src", "tm")),
        P(None, ("src", "tm")),
        P(None, ("src", "tm")),
        P(None, ("src", "tm")),
        P(None, ("src", "tm")),
        P(None, "tm", "src"),
        P(None, ("src", "tm")),
        P(None, "tm", "src"),
        P(None, ("src", "tm")),
        P(None, "tm", "src"),
        P(),
    )
    out_specs = (
        P(None, ("src", "tm")),
        P(None, ("src", "tm")),
        P(None, "tm", "src"),
        P(None, ("src", "tm")),
        P(None, "tm", "src"),
        P(None, ("src", "tm")),
        P(None, "tm", "src"),
        P(),
    )
    return jax.shard_map(shards, mesh=mesh, in_specs=in_specs, out_specs=out_specs, check_vma=False)
```

profile of v0, /device:TPU:1, one launch (start us, length us, event | category | flops | bytes accessed | tf_op | source)
XLA Modules:
  0.0 866.1 jit_solution(7644518561160794615)
XLA Ops:
  7.2 0.0 copy-start.8
  7.2 71.3 %all-gather = f32[3,1,16384]{2,1,0:T(1,128)S(1)} all-gather(f32[3,1,256]{2,1,0:T(1,128)} %param.20), channel_id=2, replica_groups=mesh['src'=64,'tm'=8] {'src'}, dimensions={2}, use_global_device_ids=true | all-gather | bytes 199680 | tf_op jit(solution)/shard_map/all_gather | solution.py:50
  78.5 0.1 fusion.2
  78.6 0.1 copy.62
  78.7 135.5 %gather_fusion.1 = f32[24576]{0:T(1024)S(1)} fusion(f32[49152]{0:T(1024)S(1)} %bitcast.46, s32[24576]{0:T(1024)S(1)} %broadcast_clamp_fusion), kind=kCustom, calls=%fused_computation.1 | custom fusion | bytes 294912 | tf_op jit(solution)/shard_map/jit(_take)/gather | solution.py:52
  214.2 0.0 copy-start
  214.3 0.8 copy-done
  215.1 0.1 multiply_reduce_fusion
  215.2 0.6 all_to_all.14
  215.8 23.8 %all-to-all-start = ((f32[8,1,256]{2,1,0:T(1,128)}), f32[8,1,256]{2,1,0:T(1,128)S(1)}, u32[]{:S(2)}, u32[]{:S(2)}) async-start(f32[8,1,256]{2,1,0:T(1,128)} %all_to_all.14), calls=%async_computation | async-start | bytes 16384 | tf_op jit(solution)/shard_map/all_to_all | solution.py:53
  239.7 0.1 broadcast_add_fusion
  239.7 0.7 copy-done.1
  240.4 0.2 copy.52
  240.6 0.5 copy-done.5
  241.2 5.5 gather_fusion
  246.7 0.0 copy-start.10
  246.7 0.3 copy.53
  247.0 0.1 add.175
  247.1 0.0 copy-start.2
  247.1 0.1 compare_select_fusion
  247.2 0.7 copy-done.2
  247.9 0.6 fusion.10
  249.8 0.0 copy-start.13
  249.8 0.7 copy-done.9
  250.5 1.3 multiply_reduce_fusion.3
  251.8 101.1 %psum.21 = f32[]{:T(128)} all-reduce(f32[]{:T(128)} %get-tuple-element.34), channel_id=1, replica_groups=mesh['src'=64,'tm'=8] {'src','tm'}, use_global_device_ids=true, to_apply=%region_3.4 | all-reduce | flops 1 | bytes 8 | tf_op jit(solution)/shard_map/psum | solution.py:56
  353.6 0.6 copy.56
  354.2 4.0 all-to-all-start.1
  358.2 4.6 all-to-all-done.1
  362.8 0.1 copy.63
  362.9 128.4 %scatter_custom_fusion.1 = f32[49152]{0:T(1024)S(1)} fusion(s32[24576]{0:T(1024)S(1)} %bitcast.50, f32[24576]{0:T(1024)S(1)} %bitcast.51, f32[]{:T(128)} %constant.77.clone.1), kind=kCustom, calls=%fused_computation.11 | custom fusion | flops 24576 | bytes 196612 | tf_op jit(solution)/shard_map/scatter-add | solution.py:67
  491.3 0.8 reshape.152
  492.1 0.0 all-reduce.2.cloned.1.call-update
  492.9 0.4 copy.58
  493.3 11.6 %scatter_custom_fusion = f32[5,1024]{0,1:T(8,128)S(1)} fusion(s32[2048]{0:T(1024)S(1)} %bitcast.55, f32[2048,5]{1,0:T(8,128)S(1)} %bitcast.48, f32[]{:T(128)} %constant.77.clone.1), kind=kCustom, calls=%fused_computation.7 | custom fusion | flops 10240 | bytes 20484 | tf_op jit(solution)/shard_map/scatter-add | solution.py:62
  504.9 0.2 copy.55
  505.8 0.0 copy-start.4
  505.8 0.6 multiply_reduce_fusion.2
  506.4 236.0 %all-reduce.2.cloned.1.call-done = f32[3,16384]{1,0:T(4,128)} async-done(((f32[3,16384]{1,0:T(4,128)}), f32[3,16384]{1,0:T(4,128)}) %all-reduce.2.cloned.1.call-update) | async-done | bytes 196624 | tf_op jit(solution)/shard_map/psum | solution.py:70
  742.4 1.3 multiply_reduce_fusion.4
  745.6 109.7 %psum.23 = f32[]{:T(128)} all-reduce(f32[]{:T(128)S(6)} %add.179), channel_id=1, replica_groups=mesh['src'=64,'tm'=8] {'src','tm'}, use_global_device_ids=true, to_apply=%region_9.10 | all-reduce | flops 1 | bytes 8 | tf_op jit(solution)/shard_map/psum | solution.py:77
  856.1 0.7 broadcast_divide_fusion.2
  856.8 0.6 broadcast_in_dim.37
  857.4 0.7 multiply_subtract_fusion
  858.1 0.0 copy-done.11
  858.1 0.0 copy-done.12
  858.1 0.6 multiply_add_fusion.1
  858.7 0.6 pad_maximum_fusion
  (31 shorter events, 0.2 us)
Async XLA Ops:
  7.2 71.3 %copy-start.8 = (s32[8,256]{1,0:T(8,128)S(1)}, s32[8,256]{1,0:T(8,128)}, u32[]{:S(2)}) copy-start(s32[8,256]{1,0:T(8,128)} %param.17) | copy-start | bytes 24580
  214.2 0.9 copy-start
  215.8 34.0 %all-to-all-start = ((f32[8,1,256]{2,1,0:T(1,128)}), f32[8,1,256]{2,1,0:T(1,128)S(1)}, u32[]{:S(2)}, u32[]{:S(2)}) async-start(f32[8,1,256]{2,1,0:T(1,128)} %all_to_all.14), calls=%async_computation | async-start | bytes 16384 | tf_op jit(solution)/shard_map/all_to_all | solution.py:53
  239.7 0.8 copy-start.1
  240.4 0.7 copy-start.5
  246.7 1.3 copy-start.10
  247.1 0.8 copy-start.2
  249.8 0.7 copy-start.9
  249.8 0.7 copy-start.13
  354.2 8.6 all-to-all-start.1
  358.2 384.2 %all-reduce.2.cloned.1.call-start = ((), (), s32[]{:S(2)}) async-start(), calls=%async_computation.2 | async-start | bytes 524288 | tf_op jit(solution)/shard_map/psum | solution.py:70
  358.2 134.0 %copy-start.6 = (f32[8,256]{1,0:T(8,128)}, f32[8,256]{1,0:T(8,128)S(1)}, u32[]{:S(2)}) copy-start(f32[8,256]{1,0:T(8,128)S(1)} %broadcast_divide_fusion.1) | copy-start | bytes 24580
  505.8 236.6 %copy-start.7 = (f32[3,1,256]{2,1,0:T(1,128)S(1)}, f32[3,1,256]{2,1,0:T(1,128)}, u32[]{:S(2)}) copy-start(f32[3,1,256]{2,1,0:T(1,128)} %param.20) | copy-start | bytes 9220
  505.8 351.6 %copy-start.4 = (f32[5,1024]{1,0:T(8,128)S(1)}, f32[5,1024]{1,0:T(8,128)}, u32[]{:S(2)}) copy-start(f32[5,1024]{1,0:T(8,128)} %param.23) | copy-start | bytes 61444
  506.4 351.0 %copy-start.3 = (f32[5,1024]{1,0:T(8,128)S(1)}, f32[5,1024]{1,0:T(8,128)}, u32[]{:S(2)}) copy-start(f32[5,1024]{1,0:T(8,128)} %param.21) | copy-start | bytes 61444
  857.4 0.7 copy-start.11
  857.4 0.7 copy-start.12
Sparse Core Ops, SparseCore 0:
  492.3 250.0 all-reduce.1
where the time goes:
time: 867 us; the launch traced here: 866 us
  blocking collectives  282 us (33%)
  waiting for transfers between devices  241 us (28%)
  local copies, waits for them, and re-layouts  149 us (17%)
  other arithmetic  146 us (17%)
  starting transfers between devices  27.8 us (3%)
  between operations  20.4 us (2%)
    psum x1, waiting for transfers between devices, shards(): knot_totals = lax.psum(knot_terms, 'src')  236 us
    gather x2, local copies, waits for them, and re-layouts, shards(): knot_image = jnp.sum(knot_coeffs * jnp.take(slab_whole, positions), axis=0)  136 us
    scatter-add x1, other arithmetic, shards(): knot_terms = jnp.zeros((3 * knots_slab,), jnp.float32).at[positions.resha...  128 us
    psum x1, blocking collectives, shards(): alpha_next = jnp.sqrt(lax.psum(squares, ('src', 'tm')) / unknowns + EPSILON)  110 us
    psum x1, blocking collectives, shards(): beta = jnp.sqrt(lax.psum(own_squares, ('src', 'tm')) / total_obs + EPSILON)  101 us
    all_gather x1, blocking collectives, shards(): lax.all_gather(own_knots, 'src', axis=1, tiled=True).reshape(-1)  71.3 us
    all_to_all x1, starting transfers between devices, shards(): lax.all_to_all(knot_image, 'tm', split_axis=0, concat_axis=0, tiled=True)  23.8 us
  transfers between devices with their start and end apart: 3, of which 2 were waited for; matrix products, arithmetic and copies ran while one was open for 2% of the time, Pallas kernels for 0%

commit v1 on v0

--- a/solution.py
+++ b/solution.py
@@ -5,6 +5,11 @@
 
 KB = 4
 EPSILON = 1e-06
+
+
+def gather_from_all(array, axis, dim):
+    copies = jnp.concatenate([array] * lax.axis_size(axis), axis=dim)
+    return lax.all_to_all(copies, axis, dim, dim, tiled=True)
 
 
 def band_positions(band_start, knots_slab):
@@ -47,7 +52,7 @@
     picked = jnp.take(source_vector, flat_source, axis=1).reshape(5, buckets, capacity)
     image = jnp.sum(source_coeffs * picked, axis=0)
     own_knots = knot_vector[:, 0, :]
-    slab_whole = lax.all_gather(own_knots, "src", axis=1, tiled=True).reshape(-1)
+    slab_whole = gather_from_all(own_knots, "src", 1).reshape(-1)
     positions = band_positions(band_start, knots_slab)
     knot_image = jnp.sum(knot_coeffs * jnp.take(slab_whole, positions), axis=0)
     returned = lax.all_to_all(knot_image, "tm", split_axis=0, concat_axis=0, tiled=True)

time: 867 us -> 811 us (0.935)
  blocking collectives: 282 us -> 209 us
  waiting for transfers between devices: 241 us -> 252 us
    all_gather x1 -> x0, blocking collectives: 71.3 us -> none  [shards(): lax.all_gather(own_knots, 'src', axis=1, tiled=True).reshape(-1)]
    all_to_all x0 -> x1, starting transfers between devices: none -> 19.2 us  [gather_from_all(): return lax.all_to_all(copies, axis, dim, dim, tiled=True)]
    all_to_all x1, starting transfers between devices: 23.8 us -> 8.38 us  [shards(): lax.all_to_all(knot_image, 'tm', split_axis=0, concat_axis=0, tiled=True)]
    all_to_all x0 -> x1, waiting for transfers between devices: none -> 11.1 us  [gather_from_all(): return lax.all_to_all(copies, axis, dim, dim, tiled=True)]
  transfers between devices with their start and end apart: 3 -> 4, of which waited for: 2 -> 4; matrix products, arithmetic and copies ran while one was open for 2% -> 2% of each run, Pallas kernels for 0% -> 0%
where the time goes in v1:
time: 811 us; the launch traced here: 810 us
  waiting for transfers between devices  252 us (31%)
  blocking collectives  209 us (26%)
  local copies, waits for them, and re-layouts  150 us (18%)
  other arithmetic  146 us (18%)
  starting transfers between devices  31.5 us (4%)
  between operations  20.4 us (3%)
    psum x1, waiting for transfers between devices, shards(): knot_totals = lax.psum(knot_terms, 'src')  234 us
    gather x2, local copies, waits for them, and re-layouts, shards(): knot_image = jnp.sum(knot_coeffs * jnp.take(slab_whole, positions), axis=0)  136 us
    scatter-add x1, other arithmetic, shards(): knot_terms = jnp.zeros((3 * knots_slab,), jnp.float32).at[positions.resha...  128 us
    psum x1, blocking collectives, shards(): alpha_next = jnp.sqrt(lax.psum(squares, ('src', 'tm')) / unknowns + EPSILON)  110 us
    psum x1, blocking collectives, shards(): beta = jnp.sqrt(lax.psum(own_squares, ('src', 'tm')) / total_obs + EPSILON)  99.4 us
    all_to_all x1, starting transfers between devices, gather_from_all(): return lax.all_to_all(copies, axis, dim, dim, tiled=True)  19.2 us
  transfers between devices with their start and end apart: 4, of which 4 were waited for; matrix products, arithmetic and copies ran while one was open for 2% of the time, Pallas kernels for 0%

profile of v1, /device:TPU:1, one launch (start us, length us, event | category | flops | bytes accessed | tf_op | source)
XLA Modules:
  0.0 809.8 jit_solution(12406862966683188085)
XLA Ops:
  7.2 0.7 copy.85
  7.9 0.7 concatenate.4
  8.6 19.2 %all-to-all-start = ((f32[3,64,256]{2,0,1:T(4,128)}), f32[3,64,256]{2,0,1:T(4,128)S(1)}, u32[]{:S(2)}, u32[]{:S(2)}) async-start(f32[3,64,256]{2,0,1:T(4,128)} %concatenate.4), calls=%async_computation | async-start | bytes 524288 | tf_op jit(solution)/shard_map/all_to_all | solution.py:12
  27.9 0.1 fusion.2
  27.9 0.0 copy-start.1
  28.0 0.1 broadcast_add_fusion
  28.0 0.7 copy-done.1
  28.7 0.2 copy.60
  28.9 0.5 copy-done.5
  29.5 5.5 gather_fusion
  34.9 0.3 copy.61
  35.3 0.1 copy.72
  35.3 0.1 add.175
  35.4 0.1 compare_select_fusion
  35.6 0.7 copy-done.2
  36.2 11.1 %all-to-all-done = f32[3,64,256]{2,0,1:T(4,128)S(1)} async-done(((f32[3,64,256]{2,0,1:T(4,128)}), f32[3,64,256]{2,0,1:T(4,128)S(1)}, u32[]{:S(2)}, u32[]{:S(2)}) %all-to-all-start) | async-done | bytes 196640 | tf_op jit(solution)/shard_map/all_to_all | solution.py:12
  47.3 0.1 copy.71
  47.5 135.5 %gather_fusion.1 = f32[24576]{0:T(1024)S(1)} fusion(f32[49152]{0:T(1024)S(1)} %bitcast.50, s32[24576]{0:T(1024)S(1)} %broadcast_clamp_fusion), kind=kCustom, calls=%fused_computation.1 | custom fusion | bytes 294912 | tf_op jit(solution)/shard_map/jit(_take)/gather | solution.py:57
  183.1 0.8 copy-done
  183.9 0.1 multiply_reduce_fusion
  184.0 0.6 all_to_all.19
  184.6 8.4 %all-to-all-start.1 = ((f32[8,1,256]{2,1,0:T(1,128)}), f32[8,1,256]{2,1,0:T(1,128)S(1)}, u32[]{:S(2)}, u32[]{:S(2)}) async-start(f32[8,1,256]{2,1,0:T(1,128)} %all_to_all.19), calls=%async_computation.1 | async-start | bytes 16384 | tf_op jit(solution)/shard_map/all_to_all | solution.py:58
  193.0 0.6 fusion.10
  194.9 2.7 all-to-all-done.1
  197.6 0.7 copy-done.13
  198.3 1.3 multiply_reduce_fusion.3
  199.6 99.4 %psum.21 = f32[]{:T(128)} all-reduce(f32[]{:T(128)} %get-tuple-element.42), channel_id=1, replica_groups=mesh['src'=64,'tm'=8] {'src','tm'}, use_global_device_ids=true, to_apply=%region_3.4 | all-reduce | flops 1 | bytes 8 | tf_op jit(solution)/shard_map/psum | solution.py:61
  299.7 0.6 copy.65
  300.3 3.9 all-to-all-start.2
  304.2 4.6 all-to-all-done.2
  308.9 0.1 copy.73
  308.9 128.4 %scatter_custom_fusion.1 = f32[49152]{0:T(1024)S(1)} fusion(s32[24576]{0:T(1024)S(1)} %bitcast.55, f32[24576]{0:T(1024)S(1)} %bitcast.56, f32[]{:T(128)} %constant.77.clone.1), kind=kCustom, calls=%fused_computation.11 | custom fusion | flops 24576 | bytes 196612 | tf_op jit(solution)/shard_map/scatter-add | solution.py:72
  437.4 0.8 reshape.284
  438.2 0.0 all-reduce.2.cloned.1.call-update
  439.0 0.4 copy.66
  439.3 11.6 %scatter_custom_fusion = f32[5,1024]{0,1:T(8,128)S(1)} fusion(s32[2048]{0:T(1024)S(1)} %bitcast.60, f32[2048,5]{1,0:T(8,128)S(1)} %bitcast.52, f32[]{:T(128)} %constant.77.clone.1), kind=kCustom, calls=%fused_computation.7 | custom fusion | flops 10240 | bytes 20484 | tf_op jit(solution)/shard_map/scatter-add | solution.py:67
  450.9 0.2 copy.64
  451.9 0.6 multiply_reduce_fusion.2
  452.5 233.6 %all-reduce.2.cloned.1.call-done = f32[3,16384]{1,0:T(4,128)} async-done(((f32[3,16384]{1,0:T(4,128)}), f32[3,16384]{1,0:T(4,128)}) %all-reduce.2.cloned.1.call-update) | async-done | bytes 196624 | tf_op jit(solution)/shard_map/psum | solution.py:75
  686.0 1.3 multiply_reduce_fusion.4
  689.3 109.7 %psum.23 = f32[]{:T(128)} all-reduce(f32[]{:T(128)S(6)} %add.179), channel_id=1, replica_groups=mesh['src'=64,'tm'=8] {'src','tm'}, use_global_device_ids=true, to_apply=%region_9.10 | all-reduce | flops 1 | bytes 8 | tf_op jit(solution)/shard_map/psum | solution.py:82
  799.8 0.7 broadcast_divide_fusion.2
  800.4 0.6 broadcast_in_dim.37
  801.0 0.7 multiply_subtract_fusion
  801.7 0.0 copy-done.11
  801.7 0.0 copy-done.12
  801.7 0.6 multiply_add_fusion.1
  802.3 0.6 pad_maximum_fusion
  (36 shorter events, 0.2 us)
Async XLA Ops:
  8.6 19.3 %copy-start.8 = (s32[8,256]{1,0:T(8,128)S(1)}, s32[8,256]{1,0:T(8,128)}, u32[]{:S(2)}) copy-start(s32[8,256]{1,0:T(8,128)} %param.17) | copy-start | bytes 24580
  8.6 38.7 %all-to-all-start = ((f32[3,64,256]{2,0,1:T(4,128)}), f32[3,64,256]{2,0,1:T(4,128)S(1)}, u32[]{:S(2)}, u32[]{:S(2)}) async-start(f32[3,64,256]{2,0,1:T(4,128)} %concatenate.4), calls=%async_computation | async-start | bytes 524288 | tf_op jit(solution)/shard_map/all_to_all | solution.py:12
  27.9 0.8 copy-start.1
  28.7 0.7 copy-start.5
  35.4 0.8 copy-start.2
  47.5 145.6 %copy-start.10 = (f32[3]{0:T(128)S(1)}, f32[3]{0:T(128)}, u32[]{:S(2)}) copy-start(f32[3]{0:T(128)} %param.25) | copy-start | bytes 40
  183.0 0.9 copy-start
  184.6 13.0 %all-to-all-start.1 = ((f32[8,1,256]{2,1,0:T(1,128)}), f32[8,1,256]{2,1,0:T(1,128)S(1)}, u32[]{:S(2)}, u32[]{:S(2)}) async-start(f32[8,1,256]{2,1,0:T(1,128)} %all_to_all.19), calls=%async_computation.1 | async-start | bytes 16384 | tf_op jit(solution)/shard_map/all_to_all | solution.py:58
  194.9 2.7 copy-start.9
  197.6 0.7 copy-start.13
  300.3 8.5 %all-to-all-start.2 = ((f32[8,1,256]{2,1,0:T(1,128)}), f32[8,1,256]{2,1,0:T(1,128)S(1)}, u32[]{:S(2)}, u32[]{:S(2)}) async-start(f32[8,1,256]{2,1,0:T(1,128)} %copy.65), calls=%async_computation.2 | async-start | bytes 16384 | tf_op jit(solution)/shard_map/all_to_all | solution.py:63
  304.2 381.8 %all-reduce.2.cloned.1.call-start = ((), (), s32[]{:S(2)}) async-start(), calls=%async_computation.3 | async-start | bytes 524288 | tf_op jit(solution)/shard_map/psum | solution.py:75
  304.2 134.0 %copy-start.6 = (f32[8,256]{1,0:T(8,128)}, f32[8,256]{1,0:T(8,128)S(1)}, u32[]{:S(2)}) copy-start(f32[8,256]{1,0:T(8,128)S(1)} %broadcast_divide_fusion.1) | copy-start | bytes 24580
  451.8 234.2 %copy-start.7 = (f32[3,1,256]{2,1,0:T(1,128)S(1)}, f32[3,1,256]{2,1,0:T(1,128)}, u32[]{:S(2)}) copy-start(f32[3,1,256]{2,1,0:T(1,128)} %param.20) | copy-start | bytes 9220
  451.8 349.2 %copy-start.4 = (f32[5,1024]{1,0:T(8,128)S(1)}, f32[5,1024]{1,0:T(8,128)}, u32[]{:S(2)}) copy-start(f32[5,1024]{1,0:T(8,128)} %param.23) | copy-start | bytes 61444
  452.5 348.6 %copy-start.3 = (f32[5,1024]{1,0:T(8,128)S(1)}, f32[5,1024]{1,0:T(8,128)}, u32[]{:S(2)}) copy-start(f32[5,1024]{1,0:T(8,128)} %param.21) | copy-start | bytes 61444
  801.0 0.7 copy-start.11
  801.0 0.7 copy-start.12
Sparse Core Ops, SparseCore 0:
  438.3 247.6 all-reduce.1
